TPU v7x, 128 devices: a whole 4x4x4 slice. The times are simulated.
128 devices in a mesh: ctx: 16 (over y, z_hi, core), tp: 8 (over z_lo, x).
Axes of the slice: x: 4, y: 4, z: 4 (z_hi: 2, z_lo: 2; z = z_hi * 2 + z_lo), core: 2. Of those that a mesh axis runs over, the one named last changes fastest.
Arguments:
- prompt_states: bfloat16 [2048, 1024], P('ctx'), may hold values from -1.5 to 1.5
- segment_ids: int32 [2048], P('ctx'), may hold values from 0 to 3, never falling along the last dimension, each value on 1 to 1024 neighbouring positions
- past_keys: bfloat16 [2048, 1024], P('ctx', 'tp'), may hold values from -1024 to 1024
- past_values: bfloat16 [2048, 1024], P('ctx', 'tp'), may hold values from -6 to 6
- cache_request: int32 [2048], P('ctx'), may hold values from 0 to 2, as said below
- decode_ids: int32 [4], replicated, may hold values from 0 to 32127
- embed_table: bfloat16 [32128, 1024], P(('ctx', 'tp')), may hold values from -6 to 6
- attn_gain: bfloat16 [1024], replicated, may hold values from 0.25 to 1.75
- ff_gain: bfloat16 [1024], replicated, may hold values from 0.25 to 1.75
- final_gain: bfloat16 [1024], replicated, may hold values from 0.25 to 1.75
- w_query: bfloat16 [1024, 1024], P(None, 'tp'), may hold values from -0.1875 to 0.1875
- w_key: bfloat16 [1024, 1024], P(None, 'tp'), may hold values from -0.1875 to 0.1875
- w_value: bfloat16 [1024, 1024], P(None, 'tp'), may hold values from -0.1875 to 0.1875
- w_out: bfloat16 [1024, 1024], P('tp'), may hold values from -0.1875 to 0.1875
- w_gate: bfloat16 [1024, 2816], P(None, 'tp'), may hold values from -0.1875 to 0.1875
- w_up: bfloat16 [1024, 2816], P(None, 'tp'), may hold values from -0.1875 to 0.1875
- w_down: bfloat16 [2816, 1024], P('tp'), may hold values from -0.109375 to 0.109375
- lm_head: bfloat16 [1024, 32128], P(None, ('ctx', 'tp')), may hold values from -0.1875 to 0.1875
Outputs:
- prompt_out: bfloat16 [2048, 1024], P('ctx')
- logits: float32 [4, 32128], P(None, ('ctx', 'tp'))
- relaid_keys: bfloat16 [2048, 1024], P(('ctx', 'tp'))
- relaid_values: bfloat16 [2048, 1024], P(('ctx', 'tp'))
Inputs may be any that keep to these rules, and one draw needn't show every extreme that they name: `cache_request`: only the even requests have cached rows, which may lie on any devices. `segment_ids`: the tokens of a request are consecutive; a request holds at most 1024 of them, and one request holds exactly that many.
All inputs are finite; a program needn't handle non-finite values.
Results may differ from a plain program's by a relative error of at most 0.03.
Values may be sent and summed in bfloat16 or wider, within the bound.
A program may use at most 64 MiB of HBM per device.

v0:
```python
import jax
import jax.numpy as jnp
from jax import lax
from jax.sharding import PartitionSpec as P

DH = 64
epsilon = 1e-06
scale_factor = 0.125
negative = -1e30


def joined(part, axis, combine):
    gathered = jax.tree.map(lambda a: lax.all_gather(a, axis), part)

    def take(source):
        return jax.tree.map(lambda a: lax.dynamic_index_in_dim(a, source, 0, False), gathered)

    return lax.fori_loop(
        1, lax.axis_size(axis), lambda source, state: combine(state, take(source)), take(0)
    )


def rms_norm(states, gain):
    states = states.astype(jnp.float32)
    mean_square = jnp.mean(states * states, axis=-1, keepdims=True)
    return (states * lax.rsqrt(mean_square + epsilon) * gain.astype(jnp.float32)).astype(
        jnp.bfloat16
    )


def partial_attend(queries, keys, values, allowed):
    scores = (
        jnp.einsum("qhd,khd->qhk", queries, keys, preferred_element_type=jnp.float32) * scale_factor
    )
    scores = jnp.where(allowed[:, None, :], scores, negative)
    highest = jnp.max(scores, axis=2)
    weights = jnp.where(allowed[:, None, :], jnp.exp(scores - highest[:, :, None]), 0.0)
    weight_sum = jnp.sum(weights, axis=2)
    summed = jnp.einsum(
        "qhk,khd->qhd", weights.astype(jnp.bfloat16), values, preferred_element_type=jnp.float32
    )
    return (highest, weight_sum, summed)


def join_parts(earlier, latter):
    highest = jnp.maximum(earlier[0], latter[0])
    left_scale = jnp.exp(earlier[0] - highest)
    right_scale = jnp.exp(latter[0] - highest)
    weight_sum = earlier[1] * left_scale + latter[1] * right_scale
    summed = earlier[2] * left_scale[:, :, None] + latter[2] * right_scale[:, :, None]
    return (highest, weight_sum, summed)


def finish(partials):
    return (partials[2] / partials[1][:, :, None]).astype(jnp.bfloat16)


def fold_block(running, query_heads, block_keys, block_values, allowed):
    key_count = block_keys.shape[0]
    head_group = query_heads.shape[1]

    def attend(current):
        return join_parts(
            current,
            partial_attend(
                query_heads,
                block_keys.reshape(key_count, head_group, DH),
                block_values.reshape(key_count, head_group, DH),
                allowed,
            ),
        )

    def unchanged(current):
        return current

    return lax.cond(jnp.any(allowed), attend, unchanged, running)


def gated_units(normed, w_gate, w_up, w_down):
    gate_value = jnp.dot(normed, w_gate, preferred_element_type=jnp.float32)
    up_value = jnp.dot(normed, w_up, preferred_element_type=jnp.float32)
    hidden = (jax.nn.gelu(gate_value, approximate=True) * up_value).astype(jnp.bfloat16)
    return jnp.dot(hidden, w_down, preferred_element_type=jnp.float32)


def project(normed, weight):
    return jnp.dot(normed, weight, preferred_element_type=jnp.float32).astype(jnp.bfloat16)


def on_device(
    prompt_states,
    segment_ids,
    past_keys,
    past_values,
    cache_request,
    decode_ids,
    embed_table,
    attn_gain,
    ff_gain,
    final_gain,
    w_query,
    w_key,
    w_value,
    w_out,
    w_gate,
    w_up,
    w_down,
    lm_head,
):
    row_count = prompt_states.shape[0]
    head_group = w_query.shape[1] // DH
    ctx_index = lax.axis_index("ctx")
    normed = rms_norm(prompt_states, attn_gain)
    queries = project(normed, w_query)
    keys = project(normed, w_key)
    values = project(normed, w_value)
    query_heads = queries.reshape(row_count, head_group, DH)
    q_positions = ctx_index * row_count + jnp.arange(row_count, dtype=jnp.int32)
    start_parts = (
        jnp.full((row_count, head_group), negative, jnp.float32),
        jnp.zeros((row_count, head_group), jnp.float32),
        jnp.zeros((row_count, head_group, DH), jnp.float32),
    )
    block_keys = lax.all_gather(keys, "ctx", axis=0, tiled=True)
    block_values = lax.all_gather(values, "ctx", axis=0, tiled=True)
    block_segment = lax.all_gather(segment_ids, "ctx", axis=0, tiled=True)
    key_positions = jnp.arange(block_segment.shape[0], dtype=jnp.int32)
    partials = fold_block(
        start_parts,
        query_heads,
        block_keys,
        block_values,
        (segment_ids[:, None] == block_segment[None, :])
        & (key_positions[None, :] <= q_positions[:, None]),
    )
    block_keys = lax.all_gather(past_keys, "ctx", axis=0, tiled=True)
    block_values = lax.all_gather(past_values, "ctx", axis=0, tiled=True)
    block_segment = lax.all_gather(cache_request, "ctx", axis=0, tiled=True)
    partials = fold_block(
        partials,
        query_heads,
        block_keys,
        block_values,
        segment_ids[:, None] == block_segment[None, :],
    )
    attended = finish(partials).reshape(row_count, head_group * DH)
    head_term = jnp.dot(attended, w_out, preferred_element_type=jnp.float32)
    residual = prompt_states.astype(jnp.float32) + lax.psum(
        head_term.astype(jnp.bfloat16), "tp"
    ).astype(jnp.float32)
    unit_term = gated_units(rms_norm(residual, ff_gain), w_gate, w_up, w_down)
    prompt_out = (
        residual + lax.psum(unit_term.astype(jnp.bfloat16), "tp").astype(jnp.float32)
    ).astype(jnp.bfloat16)
    relaid_keys, relaid_values = (
        lax.all_to_all(keys, "tp", split_axis=0, concat_axis=1, tiled=True),
        lax.all_to_all(values, "tp", split_axis=0, concat_axis=1, tiled=True),
    )
    vocab_rows = embed_table.shape[0]
    vocab_start = lax.axis_index(("ctx", "tp")) * vocab_rows
    one_hot = (
        decode_ids[:, None] == vocab_start + jnp.arange(vocab_rows, dtype=jnp.int32)[None, :]
    ).astype(jnp.bfloat16)
    embedded = lax.psum(
        jnp.dot(one_hot, embed_table, preferred_element_type=jnp.float32), ("ctx", "tp")
    )
    request_count = decode_ids.shape[0]
    decode_normed = rms_norm(embedded, attn_gain)
    decode_queries = project(decode_normed, w_query)
    decode_heads = decode_queries.reshape(request_count, head_group, DH)
    decode_keys = project(decode_normed, w_key).reshape(request_count, head_group, DH)
    decode_values = project(decode_normed, w_value).reshape(request_count, head_group, DH)
    requests = jnp.arange(request_count, dtype=jnp.int32)
    cache_count = past_keys.shape[0]
    cache_part = partial_attend(
        decode_heads,
        past_keys.reshape(cache_count, head_group, DH),
        past_values.reshape(cache_count, head_group, DH),
        requests[:, None] == cache_request[None, :],
    )
    prompt_part = partial_attend(
        decode_heads,
        keys.reshape(row_count, head_group, DH),
        values.reshape(row_count, head_group, DH),
        requests[:, None] == segment_ids[None, :],
    )
    gathered = joined(join_parts(prompt_part, cache_part), "ctx", join_parts)
    own_part = partial_attend(
        decode_heads, decode_keys, decode_values, requests[:, None] == requests[None, :]
    )
    decode_attended = finish(join_parts(gathered, own_part)).reshape(request_count, head_group * DH)
    decode_residual = embedded + lax.psum(
        jnp.dot(decode_attended, w_out, preferred_element_type=jnp.float32), "tp"
    )
    decode_term = gated_units(rms_norm(decode_residual, ff_gain), w_gate, w_up, w_down)
    decode_final = decode_residual + lax.psum(decode_term, "tp")
    logits = jnp.dot(
        rms_norm(decode_final, final_gain), lm_head, preferred_element_type=jnp.float32
    )
    return (prompt_out, logits, relaid_keys, relaid_values)


def solution(mesh):
    placed = (
        P("ctx", None),
        P("ctx"),
        P("ctx", "tp"),
        P("ctx", "tp"),
        P("ctx"),
        P(),
        P(("ctx", "tp"), None),
        P(),
        P(),
        P(),
        P(None, "tp"),
        P(None, "tp"),
        P(None, "tp"),
        P("tp", None),
        P(None, "tp"),
        P(None, "tp"),
        P("tp", None),
        P(None, ("ctx", "tp")),
    )
    return jax.shard_map(
        on_device,
        mesh=mesh,
        in_specs=placed,
        out_specs=(
            P("ctx", None),
            P(None, ("ctx", "tp")),
            P(("ctx", "tp"), None),
            P(("ctx", "tp"), None),
        ),
        check_vma=False,
    )
```

profile of v0, /device:TPU:0, one launch (start us, length us, event | category | flops | bytes accessed | tf_op | source)
XLA Modules:
  0.0 462.5 jit_solution(8723615287294162902)
XLA Ops:
  7.3 25.5 %all-gather.2 = s32[16,1,128]{2,1,0:T(1,128)S(1)} all-gather(s32[1,1,128]{2,1,0:T(1,128)} %bitcast.173), channel_id=1, replica_groups=mesh['ctx'=16,'tp'=8] {'ctx'}, dimensions={0}, use_global_device_ids=true | all-gather | bytes 8704 | tf_op jit(solution)/shard_map/all_gather | solution.py:126
  32.8 19.3 %all-gather.1 = s32[16,1,128]{2,1,0:T(1,128)S(1)} all-gather(s32[1,1,128]{2,1,0:T(1,128)} %bitcast.174), channel_id=1, replica_groups=mesh['ctx'=16,'tp'=8] {'ctx'}, dimensions={0}, use_global_device_ids=true | all-gather | bytes 8704 | tf_op jit(solution)/shard_map/all_gather | solution.py:138
  52.1 3.4 fusion.125
  58.5 1.9 convolution_convert_fusion.4
  60.5 23.8 %all_gather.34 = bf16[2048,128]{1,0:T(8,128)(2,1)S(1)} all-gather(bf16[128,128]{1,0:T(8,128)(2,1)} %convolution_convert_fusion.4), channel_id=1, replica_groups=mesh['ctx'=16,'tp'=8] {'ctx'}, dimensions={0}, use_global_device_ids=true | all-gather | bytes 557056 | tf_op jit(solution)/shard_map/all_gather | solution.py:124
  85.5 22.3 %all_gather.35 = bf16[2048,128]{1,0:T(8,128)(2,1)} all-gather(bf16[128,128]{1,0:T(8,128)(2,1)} %convolution_convert_fusion.2), channel_id=1, replica_groups=mesh['ctx'=16,'tp'=8] {'ctx'}, dimensions={0}, use_global_device_ids=true | all-gather | bytes 557056 | tf_op jit(solution)/shard_map/all_gather | solution.py:125
  108.0 25.2 %all_gather.36 = bf16[2048,128]{0,1:T(8,128)(2,1)} all-gather(bf16[128,128]{0,1:T(8,128)(2,1)S(1)} %copy.75), channel_id=1, replica_groups=mesh['ctx'=16,'tp'=8] {'ctx'}, dimensions={0}, use_global_device_ids=true | all-gather | bytes 557056 | tf_op jit(solution)/shard_map/all_gather | solution.py:136
  133.3 22.1 %all_gather.37 = bf16[2048,128]{0,1:T(8,128)(2,1)} all-gather(bf16[128,128]{0,1:T(8,128)(2,1)S(1)} %copy.76), channel_id=1, replica_groups=mesh['ctx'=16,'tp'=8] {'ctx'}, dimensions={0}, use_global_device_ids=true | all-gather | bytes 557056 | tf_op jit(solution)/shard_map/all_gather | solution.py:137
  155.4 8.3 %conditional.2 = (f32[128,2]{0,1:T(2,128)}, f32[128,2]{0,1:T(2,128)S(1)}, f32[128,2,64]{0,2,1:T(8,128)S(1)}) conditional(s32[]{:T(128)} %convert_element_type.99, () %tuple.45, (pred[128,2048]{0,1:T(8,128)(4,1)}, bf16[2048,128]{1,0:T(8,128)(2,1)S(1)}, bf16[128,2,64]{0,2,1:T(8,128)(2,1)S(1)}, bf16[2048,128]{1,0:T(8,128)(2,1)}) %tuple.100), branch_computations={%region_3.4_spmd, %region_4.7_spmd} | conditional | flops 138970624 | bytes 11384884 | solution.py:76
  156.5 1.8 fusion.131
  159.9 2.1 copy.74
  163.8 3.6 conditional.3
  168.4 4.9 %all-to-all-start = ((bf16[8,16,128]{2,1,0:T(8,128)(2,1)}), bf16[8,16,128]{2,1,0:T(8,128)(2,1)S(1)}, u32[]{:S(2)}, u32[]{:S(2)}) async-start(bf16[8,16,128]{2,1,0:T(8,128)(2,1)} %bitcast.34), calls=%async_computation | async-start | bytes 65536 | tf_op jit(solution)/shard_map/all_to_all | solution.py:156
  175.4 66.9 %psum.37 = f32[4,1024]{1,0:T(4,128)S(1)} all-reduce(f32[4,1024]{1,0:T(4,128)S(1)} %fusion.70), channel_id=1, replica_groups=mesh['ctx'=16,'tp'=8] {'ctx','tp'}, use_global_device_ids=true, to_apply=%region_14.15 | all-reduce | flops 4096 | bytes 32768 | tf_op jit(solution)/shard_map/psum | solution.py:164
  246.8 22.7 %all_gather.38 = f32[16,4,2]{1,2,0:T(2,128)S(1)} all-gather(f32[1,4,2]{1,2,0:T(2,128)S(1)} %get-tuple-element.301), channel_id=1, replica_groups=mesh['ctx'=16,'tp'=8] {'ctx'}, dimensions={0}, use_global_device_ids=true | all-gather | bytes 544 | tf_op jit(solution)/shard_map/all_gather | solution.py:13
  269.5 19.2 %all_gather.39 = f32[16,4,2]{1,2,0:T(2,128)S(1)} all-gather(f32[1,4,2]{1,2,0:T(2,128)S(1)} %get-tuple-element.300), channel_id=1, replica_groups=mesh['ctx'=16,'tp'=8] {'ctx'}, dimensions={0}, use_global_device_ids=true | all-gather | bytes 544 | tf_op jit(solution)/shard_map/all_gather | solution.py:13
  289.1 22.3 %all-gather = f32[64,2,64]{2,1,0:T(2,128)S(1)} all-gather(f32[4,2,64]{2,1,0:T(2,128)S(1)} %copy.83), channel_id=2, replica_groups=mesh['ctx'=16,'tp'=8] {'ctx'}, dimensions={0}, use_global_device_ids=true | all-gather | bytes 34816 | tf_op jit(solution)/shard_map/all_gather | solution.py:13
  311.4 4.4 while.19
  316.6 31.3 %psum.38 = f32[4,1024]{1,0:T(4,128)S(1)} all-reduce(f32[4,1024]{1,0:T(4,128)S(1)} %fusion.136), channel_id=1, replica_groups=mesh['ctx'=16,'tp'=8] {'tp'}, use_global_device_ids=true, to_apply=%region_24.25 | all-reduce | flops 4096 | bytes 32768 | tf_op jit(solution)/shard_map/psum | solution.py:192
  349.0 30.6 %psum.39 = f32[4,1024]{1,0:T(4,128)S(1)} all-reduce(f32[4,1024]{1,0:T(4,128)S(1)} %fusion.42), channel_id=1, replica_groups=mesh['ctx'=16,'tp'=8] {'tp'}, use_global_device_ids=true, to_apply=%region_26.27 | all-reduce | flops 4096 | bytes 32768 | tf_op jit(solution)/shard_map/psum | solution.py:196
  384.9 3.3 all-to-all-start.1
  388.9 5.6 %all-to-all-done.1 = bf16[8,16,128]{2,1,0:T(8,128)(2,1)S(1)} async-done(((bf16[8,16,128]{2,1,0:T(8,128)(2,1)}), bf16[8,16,128]{2,1,0:T(8,128)(2,1)S(1)}, u32[]{:S(2)}, u32[]{:S(2)}) %all-to-all-start.1) | async-done | bytes 32800 | tf_op jit(solution)/shard_map/all_to_all | solution.py:157
  395.1 58.8 %all-reduce.5.cloned.1.call-done = bf16[128,1024]{1,0:T(8,128)(2,1)} async-done(((bf16[128,1024]{1,0:T(8,128)(2,1)}), bf16[128,1024]{1,0:T(8,128)(2,1)}) %all-reduce.5.cloned.1.call-update) | async-done | bytes 262160 | tf_op jit(solution)/shard_map/psum | solution.py:153
  453.9 1.8 add_convert_fusion
  (173 shorter events, 31.8 us)
Async XLA Ops:
  7.2 341.2 %copy-start = (bf16[352,1024]{1,0:T(8,128)(2,1)S(1)}, bf16[352,1024]{1,0:T(8,128)(2,1)}, u32[]{:S(2)}) copy-start(bf16[352,1024]{1,0:T(8,128)(2,1)} %param.40) | copy-start | bytes 2162692
  7.2 77.1 %copy-start.1 = (bf16[128,1024]{1,0:T(8,128)(2,1)S(1)}, bf16[128,1024]{1,0:T(8,128)(2,1)}, u32[]{:S(2)}) copy-start(bf16[128,1024]{1,0:T(8,128)(2,1)} %param.24) | copy-start | bytes 786436
  7.2 77.1 %copy-start.10 = (bf16[1024,128]{1,0:T(8,128)(2,1)S(1)}, bf16[1024,128]{1,0:T(8,128)(2,1)}, u32[]{:S(2)}) copy-start(bf16[1024,128]{1,0:T(8,128)(2,1)} %param.34) | copy-start | bytes 786436
  7.2 77.4 %copy-start.11 = (bf16[1024,128]{1,0:T(8,128)(2,1)S(1)}, bf16[1024,128]{1,0:T(8,128)(2,1)}, u32[]{:S(2)}) copy-start(bf16[1024,128]{1,0:T(8,128)(2,1)} %param.36) | copy-start | bytes 786436
  7.2 100.6 %copy-start.12 = (bf16[128,128]{1,0:T(8,128)(2,1)S(1)}, bf16[128,128]{1,0:T(8,128)(2,1)}, u32[]{:S(2)}) copy-start(bf16[128,128]{1,0:T(8,128)(2,1)} %param.26) | copy-start | bytes 98308
  7.2 373.4 %all-reduce.3.cloned.1.call-start = ((), (), s32[]{:S(2)}) async-start(), calls=%async_computation.2 | async-start | bytes 524288 | tf_op jit(solution)/shard_map/psum | solution.py:148
  55.5 77.7 %copy-start.13 = (bf16[128,128]{1,0:T(8,128)(2,1)S(1)}, bf16[128,128]{1,0:T(8,128)(2,1)}, u32[]{:S(2)}) copy-start(bf16[128,128]{1,0:T(8,128)(2,1)} %param.27) | copy-start | bytes 98308
  156.4 2.4 copy-start.5
  163.7 3.7 copy-start.6
  163.7 9.7 %copy-start.18 = (s32[128]{0:T(128)S(1)}, s32[128]{0:T(128)}, u32[]{:S(2)}) copy-start(s32[128]{0:T(128)} %param.28) | copy-start | bytes 1540
  163.7 10.5 %copy-start.16 = (s32[128]{0:T(128)S(1)}, s32[128]{0:T(128)}, u32[]{:S(2)}) copy-start(s32[128]{0:T(128)} %param.25) | copy-start | bytes 1540
  163.7 11.4 %copy-start.7 = (bf16[251,1024]{1,0:T(8,128)(2,1)S(1)}, bf16[251,1024]{1,0:T(8,128)(2,1)}, u32[]{:S(2)}) copy-start(bf16[251,1024]{1,0:T(8,128)(2,1)} %param.30) | copy-start | bytes 1542148
  163.7 11.4 %copy-start.17 = (s32[4]{0:T(128)S(1)}, s32[4]{0:T(128)}, u32[]{:S(2)}) copy-start(s32[4]{0:T(128)} %param.29) | copy-start | bytes 52
  163.8 2.9 copy-start.9
  167.4 78.5 %copy-start.14 = (bf16[1024]{0:T(1024)(128)(2,1)S(1)}, bf16[1024]{0:T(1024)(128)(2,1)}, u32[]{:S(2)}) copy-start(bf16[1024]{0:T(1024)(128)(2,1)} %param.32) | copy-start | bytes 6148
  167.4 180.7 %copy-start.3 = (bf16[1024,352]{0,1:T(8,128)(2,1)S(1)}, bf16[1024,352]{0,1:T(8,128)(2,1)}, u32[]{:S(2)}) copy-start(bf16[1024,352]{0,1:T(8,128)(2,1)} %param.38) | copy-start | bytes 2162692
  168.4 180.0 %copy-start.4 = (bf16[1024,352]{0,1:T(8,128)(2,1)S(1)}, bf16[1024,352]{0,1:T(8,128)(2,1)}, u32[]{:S(2)}) copy-start(bf16[1024,352]{0,1:T(8,128)(2,1)} %param.39) | copy-start | bytes 2162692
  168.4 216.5 %all-to-all-start = ((bf16[8,16,128]{2,1,0:T(8,128)(2,1)}), bf16[8,16,128]{2,1,0:T(8,128)(2,1)S(1)}, u32[]{:S(2)}, u32[]{:S(2)}) async-start(bf16[8,16,128]{2,1,0:T(8,128)(2,1)} %bitcast.34), calls=%async_computation | async-start | bytes 65536 | tf_op jit(solution)/shard_map/all_to_all | solution.py:156
  173.3 280.5 %all-reduce.5.cloned.1.call-start = ((), (), s32[]{:S(2)}) async-start(), calls=%async_computation.3 | async-start | bytes 524288 | tf_op jit(solution)/shard_map/psum | solution.py:153
  244.7 135.1 %copy-start.15 = (bf16[1024]{0:T(1024)(128)(2,1)S(1)}, bf16[1024]{0:T(1024)(128)(2,1)}, u32[]{:S(2)}) copy-start(bf16[1024]{0:T(1024)(128)(2,1)} %param.33) | copy-start | bytes 6148
  244.7 135.1 %copy-start.8 = (bf16[1024,251]{1,0:T(8,128)(2,1)S(1)}, bf16[1024,251]{1,0:T(8,128)(2,1)}, u32[]{:S(2)}) copy-start(bf16[1024,251]{1,0:T(8,128)(2,1)} %param.41) | copy-start | bytes 1542148
  380.6 2.6 copy-start.2
  384.9 9.5 %all-to-all-start.1 = ((bf16[8,16,128]{2,1,0:T(8,128)(2,1)}), bf16[8,16,128]{2,1,0:T(8,128)(2,1)S(1)}, u32[]{:S(2)}, u32[]{:S(2)}) async-start(bf16[8,16,128]{2,1,0:T(8,128)(2,1)} %bitcast.36), calls=%async_computation.1 | async-start | bytes 65536 | tf_op jit(solution)/shard_map/all_to_all | solution.py:157
Sparse Core Ops, SparseCore 0:
  168.5 73.1 all-reduce.2
  385.0 68.7 all-reduce.4
where the time goes:
time: 464 us; the launch traced here: 462 us
  blocking collectives  331 us (71%)
  waiting for transfers between devices  64.4 us (14%)
  matrix products  19.7 us (4%)
  between operations  15.7 us (3%)
  other arithmetic  13.4 us (3%)
  local copies, waits for them, and re-layouts  9.55 us (2%)
  starting transfers between devices  8.32 us (2%)
    psum x1, blocking collectives, on_device(): lax.psum(jnp.dot(one_hot, embed_table, preferred_element_type=jnp.float32...  66.9 us
    all_gather x3, blocking collectives, joined(): gathered = jax.tree.map(lambda a: lax.all_gather(a, axis), part)  64.2 us
    psum x1, waiting for transfers between devices, on_device(): lax.psum(unit_term.astype(jnp.bfloat16), 'tp').astype(jnp.float32)  58.8 us
    psum x1, blocking collectives, on_device(): lax.psum(jnp.dot(decode_attended, w_out, preferred_element_type=jnp.float...  31.3 us
    psum x1, blocking collectives, on_device(): decode_final = decode_residual + lax.psum(decode_term, 'tp')  30.6 us
    all_gather x1, blocking collectives, on_device(): block_segment = lax.all_gather(segment_ids, 'ctx', axis=0, tiled=True)  25.5 us
    all_gather x1, blocking collectives, on_device(): block_keys = lax.all_gather(past_keys, 'ctx', axis=0, tiled=True)  25.2 us
    all_gather x1, blocking collectives, on_device(): block_keys = lax.all_gather(keys, 'ctx', axis=0, tiled=True)  23.8 us
  transfers between devices with their start and end apart: 4, of which 2 were waited for; matrix products, arithmetic and copies ran while one was open for 4% of the time, Pallas kernels for 0%

commit v1 on v0

--- a/solution.py
+++ b/solution.py
@@ -161,9 +161,8 @@
     one_hot = (
         decode_ids[:, None] == vocab_start + jnp.arange(vocab_rows, dtype=jnp.int32)[None, :]
     ).astype(jnp.bfloat16)
-    embedded = lax.psum(
-        jnp.dot(one_hot, embed_table, preferred_element_type=jnp.float32), ("ctx", "tp")
-    )
+    inner = lax.psum(jnp.dot(one_hot, embed_table, preferred_element_type=jnp.float32), "tp")
+    embedded = lax.psum(inner, "ctx")
     request_count = decode_ids.shape[0]
     decode_normed = rms_norm(embedded, attn_gain)
     decode_queries = project(decode_normed, w_query)

time: 464 us -> 494 us (1.065)
  blocking collectives: 331 us -> 360 us
    psum x0 -> x1, blocking collectives: none -> 64.9 us  [on_device(): embedded = lax.psum(inner, 'ctx')]
    psum x1, blocking collectives: 66.9 us -> 34.6 us  [on_device(): lax.psum(jnp.dot(one_hot, embed_table, preferred_element_type=jnp.float32...]
where the time goes in v1:
time: 494 us; the launch traced here: 493 us
  blocking collectives  360 us (73%)
  waiting for transfers between devices  66.2 us (13%)
  matrix products  19.7 us (4%)
  between operations  15.7 us (3%)
  other arithmetic  13.4 us (3%)
  local copies, waits for them, and re-layouts  9.55 us (2%)
  starting transfers between devices  8.32 us (2%)
    psum x1, blocking collectives, on_device(): embedded = lax.psum(inner, 'ctx')  64.9 us
    all_gather x3, blocking collectives, joined(): gathered = jax.tree.map(lambda a: lax.all_gather(a, axis), part)  60.8 us
    psum x1, waiting for transfers between devices, on_device(): lax.psum(unit_term.astype(jnp.bfloat16), 'tp').astype(jnp.float32)  60.6 us
    psum x1, blocking collectives, on_device(): lax.psum(jnp.dot(one_hot, embed_table, preferred_element_type=jnp.float32...  34.6 us
    psum x1, blocking collectives, on_device(): decode_final = decode_residual + lax.psum(decode_term, 'tp')  30.7 us
    psum x1, blocking collectives, on_device(): lax.psum(jnp.dot(decode_attended, w_out, preferred_element_type=jnp.float...  30.6 us
    all_gather x1, blocking collectives, on_device(): block_segment = lax.all_gather(segment_ids, 'ctx', axis=0, tiled=True)  25.5 us
    all_gather x1, blocking collectives, on_device(): block_keys = lax.all_gather(past_keys, 'ctx', axis=0, tiled=True)  25.2 us
  transfers between devices with their start and end apart: 4, of which 2 were waited for; matrix products, arithmetic and copies ran while one was open for 4% of the time, Pallas kernels for 0%

profile of v1, /device:TPU:0, one launch (start us, length us, event | category | flops | bytes accessed | tf_op | source)
XLA Modules:
  0.0 492.8 jit_solution(2330567068291193642)
XLA Ops:
  7.3 25.5 %all-gather.2 = s32[16,1,128]{2,1,0:T(1,128)S(1)} all-gather(s32[1,1,128]{2,1,0:T(1,128)} %bitcast.173), channel_id=1, replica_groups=mesh['ctx'=16,'tp'=8] {'ctx'}, dimensions={0}, use_global_device_ids=true | all-gather | bytes 8704 | tf_op jit(solution)/shard_map/all_gather | solution.py:126
  32.8 19.3 %all-gather.1 = s32[16,1,128]{2,1,0:T(1,128)S(1)} all-gather(s32[1,1,128]{2,1,0:T(1,128)} %bitcast.174), channel_id=1, replica_groups=mesh['ctx'=16,'tp'=8] {'ctx'}, dimensions={0}, use_global_device_ids=true | all-gather | bytes 8704 | tf_op jit(solution)/shard_map/all_gather | solution.py:138
  52.1 3.4 fusion.125
  58.5 1.9 convolution_convert_fusion.4
  60.5 23.8 %all_gather.34 = bf16[2048,128]{1,0:T(8,128)(2,1)S(1)} all-gather(bf16[128,128]{1,0:T(8,128)(2,1)} %convolution_convert_fusion.4), channel_id=1, replica_groups=mesh['ctx'=16,'tp'=8] {'ctx'}, dimensions={0}, use_global_device_ids=true | all-gather | bytes 557056 | tf_op jit(solution)/shard_map/all_gather | solution.py:124
  85.5 22.3 %all_gather.35 = bf16[2048,128]{1,0:T(8,128)(2,1)} all-gather(bf16[128,128]{1,0:T(8,128)(2,1)} %convolution_convert_fusion.2), channel_id=1, replica_groups=mesh['ctx'=16,'tp'=8] {'ctx'}, dimensions={0}, use_global_device_ids=true | all-gather | bytes 557056 | tf_op jit(solution)/shard_map/all_gather | solution.py:125
  108.0 25.2 %all_gather.36 = bf16[2048,128]{0,1:T(8,128)(2,1)} all-gather(bf16[128,128]{0,1:T(8,128)(2,1)S(1)} %copy.75), channel_id=1, replica_groups=mesh['ctx'=16,'tp'=8] {'ctx'}, dimensions={0}, use_global_device_ids=true | all-gather | bytes 557056 | tf_op jit(solution)/shard_map/all_gather | solution.py:136
  133.3 22.1 %all_gather.37 = bf16[2048,128]{0,1:T(8,128)(2,1)} all-gather(bf16[128,128]{0,1:T(8,128)(2,1)S(1)} %copy.76), channel_id=1, replica_groups=mesh['ctx'=16,'tp'=8] {'ctx'}, dimensions={0}, use_global_device_ids=true | all-gather | bytes 557056 | tf_op jit(solution)/shard_map/all_gather | solution.py:137
  155.4 8.3 %conditional.2 = (f32[128,2]{0,1:T(2,128)}, f32[128,2]{0,1:T(2,128)S(1)}, f32[128,2,64]{0,2,1:T(8,128)S(1)}) conditional(s32[]{:T(128)} %convert_element_type.99, () %tuple.45, (pred[128,2048]{0,1:T(8,128)(4,1)}, bf16[2048,128]{1,0:T(8,128)(2,1)S(1)}, bf16[128,2,64]{0,2,1:T(8,128)(2,1)S(1)}, bf16[2048,128]{1,0:T(8,128)(2,1)}) %tuple.100), branch_computations={%region_3.4_spmd, %region_4.7_spmd} | conditional | flops 138970624 | bytes 11384884 | solution.py:76
  156.5 1.8 fusion.131
  159.9 2.1 copy.74
  163.8 3.6 conditional.3
  168.4 4.9 all-to-all-start
  175.4 34.6 %psum.44 = f32[4,1024]{1,0:T(4,128)S(1)} all-reduce(f32[4,1024]{1,0:T(4,128)S(1)} %fusion.70), channel_id=1, replica_groups=mesh['ctx'=16,'tp'=8] {'tp'}, use_global_device_ids=true, to_apply=%region_14.15 | all-reduce | flops 4096 | bytes 32768 | tf_op jit(solution)/shard_map/psum | solution.py:164
  210.0 64.9 %psum.45 = f32[4,1024]{1,0:T(4,128)S(1)} all-reduce(f32[4,1024]{1,0:T(4,128)S(1)} %psum.44), channel_id=1, replica_groups=mesh['ctx'=16,'tp'=8] {'ctx'}, use_global_device_ids=true, to_apply=%region_15.16 | all-reduce | flops 4096 | bytes 32768 | tf_op jit(solution)/shard_map/psum | solution.py:165
  279.4 19.0 %all_gather.38 = f32[16,4,2]{1,2,0:T(2,128)S(1)} all-gather(f32[1,4,2]{1,2,0:T(2,128)S(1)} %get-tuple-element.301), channel_id=1, replica_groups=mesh['ctx'=16,'tp'=8] {'ctx'}, dimensions={0}, use_global_device_ids=true | all-gather | bytes 544 | tf_op jit(solution)/shard_map/all_gather | solution.py:13
  298.4 22.4 %all_gather.39 = f32[16,4,2]{1,2,0:T(2,128)S(1)} all-gather(f32[1,4,2]{1,2,0:T(2,128)S(1)} %get-tuple-element.300), channel_id=1, replica_groups=mesh['ctx'=16,'tp'=8] {'ctx'}, dimensions={0}, use_global_device_ids=true | all-gather | bytes 544 | tf_op jit(solution)/shard_map/all_gather | solution.py:13
  321.2 19.4 %all-gather = f32[64,2,64]{2,1,0:T(2,128)S(1)} all-gather(f32[4,2,64]{2,1,0:T(2,128)S(1)} %copy.83), channel_id=2, replica_groups=mesh['ctx'=16,'tp'=8] {'ctx'}, dimensions={0}, use_global_device_ids=true | all-gather | bytes 34816 | tf_op jit(solution)/shard_map/all_gather | solution.py:13
  340.6 4.4 while.19
  345.8 30.6 %psum.46 = f32[4,1024]{1,0:T(4,128)S(1)} all-reduce(f32[4,1024]{1,0:T(4,128)S(1)} %fusion.136), channel_id=1, replica_groups=mesh['ctx'=16,'tp'=8] {'tp'}, use_global_device_ids=true, to_apply=%region_25.26 | all-reduce | flops 4096 | bytes 32768 | tf_op jit(solution)/shard_map/psum | solution.py:191
  377.5 30.7 %psum.47 = f32[4,1024]{1,0:T(4,128)S(1)} all-reduce(f32[4,1024]{1,0:T(4,128)S(1)} %fusion.42), channel_id=1, replica_groups=mesh['ctx'=16,'tp'=8] {'tp'}, use_global_device_ids=true, to_apply=%region_27.28 | all-reduce | flops 4096 | bytes 32768 | tf_op jit(solution)/shard_map/psum | solution.py:195
  413.4 3.3 all-to-all-start.1
  417.4 5.6 %all-to-all-done.1 = bf16[8,16,128]{2,1,0:T(8,128)(2,1)S(1)} async-done(((bf16[8,16,128]{2,1,0:T(8,128)(2,1)}), bf16[8,16,128]{2,1,0:T(8,128)(2,1)S(1)}, u32[]{:S(2)}, u32[]{:S(2)}) %all-to-all-start.1) | async-done | bytes 32800 | tf_op jit(solution)/shard_map/all_to_all | solution.py:157
  423.6 60.6 %all-reduce.5.cloned.1.call-done = bf16[128,1024]{1,0:T(8,128)(2,1)} async-done(((bf16[128,1024]{1,0:T(8,128)(2,1)}), bf16[128,1024]{1,0:T(8,128)(2,1)}) %all-reduce.5.cloned.1.call-update) | async-done | bytes 262160 | tf_op jit(solution)/shard_map/psum | solution.py:153
  (174 shorter events, 33.6 us)
Async XLA Ops:
  7.2 369.7 %copy-start = (bf16[352,1024]{1,0:T(8,128)(2,1)S(1)}, bf16[352,1024]{1,0:T(8,128)(2,1)}, u32[]{:S(2)}) copy-start(bf16[352,1024]{1,0:T(8,128)(2,1)} %param.40) | copy-start | bytes 2162692
  7.2 77.1 %copy-start.1 = (bf16[128,1024]{1,0:T(8,128)(2,1)S(1)}, bf16[128,1024]{1,0:T(8,128)(2,1)}, u32[]{:S(2)}) copy-start(bf16[128,1024]{1,0:T(8,128)(2,1)} %param.24) | copy-start | bytes 786436
  7.2 77.1 %copy-start.10 = (bf16[1024,128]{1,0:T(8,128)(2,1)S(1)}, bf16[1024,128]{1,0:T(8,128)(2,1)}, u32[]{:S(2)}) copy-start(bf16[1024,128]{1,0:T(8,128)(2,1)} %param.34) | copy-start | bytes 786436
  7.2 77.4 %copy-start.11 = (bf16[1024,128]{1,0:T(8,128)(2,1)S(1)}, bf16[1024,128]{1,0:T(8,128)(2,1)}, u32[]{:S(2)}) copy-start(bf16[1024,128]{1,0:T(8,128)(2,1)} %param.36) | copy-start | bytes 786436
  7.2 100.6 %copy-start.12 = (bf16[128,128]{1,0:T(8,128)(2,1)S(1)}, bf16[128,128]{1,0:T(8,128)(2,1)}, u32[]{:S(2)}) copy-start(bf16[128,128]{1,0:T(8,128)(2,1)} %param.26) | copy-start | bytes 98308
  7.2 401.9 %all-reduce.3.cloned.1.call-start = ((), (), s32[]{:S(2)}) async-start(), calls=%async_computation.2 | async-start | bytes 524288 | tf_op jit(solution)/shard_map/psum | solution.py:148
  55.5 77.7 %copy-start.13 = (bf16[128,128]{1,0:T(8,128)(2,1)S(1)}, bf16[128,128]{1,0:T(8,128)(2,1)}, u32[]{:S(2)}) copy-start(bf16[128,128]{1,0:T(8,128)(2,1)} %param.27) | copy-start | bytes 98308
  156.4 2.4 copy-start.5
  163.7 3.7 copy-start.6
  163.7 9.7 %copy-start.18 = (s32[128]{0:T(128)S(1)}, s32[128]{0:T(128)}, u32[]{:S(2)}) copy-start(s32[128]{0:T(128)} %param.28) | copy-start | bytes 1540
  163.7 10.5 %copy-start.16 = (s32[128]{0:T(128)S(1)}, s32[128]{0:T(128)}, u32[]{:S(2)}) copy-start(s32[128]{0:T(128)} %param.25) | copy-start | bytes 1540
  163.7 11.4 %copy-start.7 = (bf16[251,1024]{1,0:T(8,128)(2,1)S(1)}, bf16[251,1024]{1,0:T(8,128)(2,1)}, u32[]{:S(2)}) copy-start(bf16[251,1024]{1,0:T(8,128)(2,1)} %param.30) | copy-start | bytes 1542148
  163.7 11.4 %copy-start.17 = (s32[4]{0:T(128)S(1)}, s32[4]{0:T(128)}, u32[]{:S(2)}) copy-start(s32[4]{0:T(128)} %param.29) | copy-start | bytes 52
  163.8 2.9 copy-start.9
  167.4 111.1 %copy-start.14 = (bf16[1024]{0:T(1024)(128)(2,1)S(1)}, bf16[1024]{0:T(1024)(128)(2,1)}, u32[]{:S(2)}) copy-start(bf16[1024]{0:T(1024)(128)(2,1)} %param.32) | copy-start | bytes 6148
  167.4 209.1 %copy-start.3 = (bf16[1024,352]{0,1:T(8,128)(2,1)S(1)}, bf16[1024,352]{0,1:T(8,128)(2,1)}, u32[]{:S(2)}) copy-start(bf16[1024,352]{0,1:T(8,128)(2,1)} %param.38) | copy-start | bytes 2162692
  168.4 208.4 %copy-start.4 = (bf16[1024,352]{0,1:T(8,128)(2,1)S(1)}, bf16[1024,352]{0,1:T(8,128)(2,1)}, u32[]{:S(2)}) copy-start(bf16[1024,352]{0,1:T(8,128)(2,1)} %param.39) | copy-start | bytes 2162692
  168.4 245.0 %all-to-all-start = ((bf16[8,16,128]{2,1,0:T(8,128)(2,1)}), bf16[8,16,128]{2,1,0:T(8,128)(2,1)S(1)}, u32[]{:S(2)}, u32[]{:S(2)}) async-start(bf16[8,16,128]{2,1,0:T(8,128)(2,1)} %bitcast.34), calls=%async_computation | async-start | bytes 65536 | tf_op jit(solution)/shard_map/all_to_all | solution.py:156
  173.3 310.9 %all-reduce.5.cloned.1.call-start = ((), (), s32[]{:S(2)}) async-start(), calls=%async_computation.3 | async-start | bytes 524288 | tf_op jit(solution)/shard_map/psum | solution.py:153
  277.3 131.0 %copy-start.15 = (bf16[1024]{0:T(1024)(128)(2,1)S(1)}, bf16[1024]{0:T(1024)(128)(2,1)}, u32[]{:S(2)}) copy-start(bf16[1024]{0:T(1024)(128)(2,1)} %param.33) | copy-start | bytes 6148
  277.3 131.0 %copy-start.8 = (bf16[1024,251]{1,0:T(8,128)(2,1)S(1)}, bf16[1024,251]{1,0:T(8,128)(2,1)}, u32[]{:S(2)}) copy-start(bf16[1024,251]{1,0:T(8,128)(2,1)} %param.41) | copy-start | bytes 1542148
  409.1 2.6 copy-start.2
  413.4 9.5 %all-to-all-start.1 = ((bf16[8,16,128]{2,1,0:T(8,128)(2,1)}), bf16[8,16,128]{2,1,0:T(8,128)(2,1)S(1)}, u32[]{:S(2)}, u32[]{:S(2)}) async-start(bf16[8,16,128]{2,1,0:T(8,128)(2,1)} %bitcast.36), calls=%async_computation.1 | async-start | bytes 65536 | tf_op jit(solution)/shard_map/all_to_all | solution.py:157
Sparse Core Ops, SparseCore 0:
  168.5 73.0 all-reduce.2
  413.5 70.6 all-reduce.4
